TPU v7x, 128 devices: a whole 4x4x4 slice. The times are simulated.
128 devices in a mesh: dp: 8 (over z, y_lo), cp: 16 (over x, y_hi, core).
Axes of the slice: x: 4, y: 4 (y_hi: 2, y_lo: 2; y = y_hi * 2 + y_lo), z: 4, core: 2. Of those that a mesh axis runs over, the one named last changes fastest.
Arguments:
- table_rows: bfloat16 [262144, 1024], P(('dp', 'cp')), may hold values from -6 to 6
- row_scales: float32 [262144], P(('dp', 'cp')), may hold values from 0.25 to 4
- owners: int32 [16384, 1], P(('dp', 'cp')), may hold values from 0 to 127; in each aligned block of 128 rows (0 to 127, 128 to 255, ...) at most 2 rows name the same one
- shard_rows: int32 [16384], P(('dp', 'cp')), may hold values from 0 to 2047
- history_lengths: int32 [8, 3], P('dp'), may hold values from 1 to 1024, 2048 in all within a row
- input_weight: bfloat16 [1024, 4096], replicated, may hold values from -0.1875 to 0.1875
- output_weight: bfloat16 [1024, 1024], replicated, may hold values from -0.1875 to 0.1875
- cotangent: bfloat16 [16384, 1024], P(('dp', 'cp')), may hold values from -6 to 6
Outputs:
- layer_out: bfloat16 [16384, 1024], P(('dp', 'cp'))
- table_grad: float32 [262144, 1024], P(('dp', 'cp'))
Inputs may be any that keep to these rules, and one draw needn't show every extreme that they name: `owners`: among the events of one device no shard is named more than 2 times, and some device names one shard exactly 2 times. `history_lengths`: the 3 lengths of a cycle group sum to 2048; the longest is exactly 1024.
All inputs are finite; a program needn't handle non-finite values.
Results may differ from a plain program's by a relative error of at most 0.0043.
Values may be sent and summed in bfloat16 or wider, within the bound.
No kernel may reach another device: no remote copies, remote signals or barrier semaphores. Data moves between devices by JAX's collectives and lax.ppermute only.
A program may use at most 128 MiB of HBM per device.

v0:
```python
import jax
import jax.numpy as jnp
from jax import lax
from jax.sharding import PartitionSpec as P

HEADS = 8
EPSILON = 1e-05


def doc_bounds(lengths, positions):
    ends_at = jnp.cumsum(lengths)
    begins_at = ends_at - lengths
    inside = (positions[:, None] >= begins_at[None, :]) & (positions[:, None] < ends_at[None, :])
    doc_first = jnp.sum(jnp.where(inside, begins_at[None, :], 0), axis=1)
    doc_length = jnp.sum(jnp.where(inside, lengths[None, :], 0), axis=1).astype(jnp.float32)
    return (doc_first, doc_length)


def normalize(values):
    center = jnp.mean(values, axis=-1, keepdims=True)
    shifted = values - center
    inv_spread = lax.rsqrt(jnp.mean(shifted * shifted, axis=-1, keepdims=True) + EPSILON)
    return (shifted * inv_spread, inv_spread)


def normalize_back(grad_in, normed, inv_spread):
    return inv_spread * (
        grad_in
        - jnp.mean(grad_in, axis=-1, keepdims=True)
        - normed * jnp.mean(grad_in * normed, axis=-1, keepdims=True)
    )


def score_block(queries, key_block, query_pos, query_first, key_pos):
    scaling = queries.shape[-1] ** (-0.5)
    scores = (
        jnp.einsum("qhe,khe->hqk", queries, key_block, preferred_element_type=jnp.float32) * scaling
    )
    allowed = (key_pos[None, :] >= query_first[:, None]) & (key_pos[None, :] <= query_pos[:, None])
    return (scores, allowed[None])


def forward_part(queries, key_block, value_block, query_pos, query_first, query_length, key_pos):
    scores, allowed = score_block(queries, key_block, query_pos, query_first, key_pos)
    weights = jnp.where(
        allowed, scores * jax.nn.sigmoid(scores) / query_length[None, :, None], 0.0
    ).astype(jnp.bfloat16)
    return jnp.einsum("hqk,khe->qhe", weights, value_block, preferred_element_type=jnp.float32)


def backward_part(
    queries, key_block, value_block, grad_out, query_pos, query_first, query_length, key_pos
):
    scores, allowed = score_block(queries, key_block, query_pos, query_first, key_pos)
    sigmoid_part = jax.nn.sigmoid(scores)
    weights = jnp.where(allowed, scores * sigmoid_part / query_length[None, :, None], 0.0).astype(
        jnp.bfloat16
    )
    grad_weights = jnp.einsum(
        "qhe,khe->hqk", grad_out, value_block, preferred_element_type=jnp.float32
    )
    silu_slope = sigmoid_part * (1.0 + scores * (1.0 - sigmoid_part))
    scaling = queries.shape[-1] ** (-0.5)
    grad_scores = jnp.where(
        allowed, grad_weights * silu_slope / query_length[None, :, None] * scaling, 0.0
    ).astype(jnp.bfloat16)
    grad_query = jnp.einsum(
        "hqk,khe->qhe", grad_scores, key_block, preferred_element_type=jnp.float32
    )
    grad_key = jnp.einsum("hqk,qhe->khe", grad_scores, queries, preferred_element_type=jnp.float32)
    grad_value = jnp.einsum("hqk,qhe->khe", weights, grad_out, preferred_element_type=jnp.float32)
    return (grad_query, grad_key, grad_value)


def sweep(kernel, running, key_total, block_size, lowest, highest):

    def advance(block_index, current):
        block_start = block_index * block_size
        needed = (block_start <= highest) & (block_start + block_size > lowest)
        return lax.cond(
            needed,
            lambda state: kernel(state, block_start, block_size),
            lambda state: state,
            current,
        )

    return lax.fori_loop(0, key_total // block_size, advance, running)


def per_device(
    table_rows,
    row_scales,
    owners,
    shard_rows,
    history_lengths,
    input_weight,
    output_weight,
    cotangent,
):
    row_count = owners.shape[0]
    model_width = table_rows.shape[1]
    head_count = HEADS
    head_size = model_width // head_count
    devices = lax.axis_size(("dp", "cp"))
    capacity = max(2, 2 * row_count // devices)
    target = owners[:, 0]
    matches = (target[:, None] == jnp.arange(devices, dtype=jnp.int32)[None, :]).astype(jnp.int32)
    before = jnp.cumsum(matches, axis=0) - matches
    ranked = jnp.sum(before * matches, axis=1)
    placed = target * capacity + ranked
    requests = jnp.zeros((devices * capacity,), jnp.int32).at[placed].set(shard_rows + 1)
    incoming = lax.all_to_all(
        requests.reshape(devices, capacity), ("dp", "cp"), split_axis=0, concat_axis=0, tiled=True
    ).reshape(-1)
    wanted = incoming > 0
    lookup = jnp.maximum(incoming - 1, 0)
    fetched = jnp.where(
        wanted[:, None], table_rows[lookup].astype(jnp.float32) * row_scales[lookup][:, None], 0.0
    )
    returned = lax.all_to_all(
        fetched.reshape(devices, capacity, model_width),
        ("dp", "cp"),
        split_axis=0,
        concat_axis=0,
        tiled=True,
    )
    embedded = returned.reshape(devices * capacity, model_width)[placed]
    normed, inv_embed = normalize(embedded)
    projected = jnp.dot(
        normed.astype(jnp.bfloat16), input_weight, preferred_element_type=jnp.float32
    )
    activated = (projected * jax.nn.sigmoid(projected)).astype(jnp.bfloat16)
    gate_rows = activated[:, :model_width]
    value_rows = activated[:, model_width : 2 * model_width]
    query_rows = activated[:, 2 * model_width : 3 * model_width]
    key_rows = activated[:, 3 * model_width :]
    lengths = history_lengths[0]
    cycle_pos = lax.axis_index("cp") * row_count + jnp.arange(row_count, dtype=jnp.int32)
    query_first, query_length = doc_bounds(lengths, cycle_pos)
    lowest = jnp.min(query_first)
    highest = cycle_pos[row_count - 1]
    key_all, value_all = (
        lax.all_gather(key_rows, "cp", axis=0, tiled=True),
        lax.all_gather(value_rows, "cp", axis=0, tiled=True),
    )
    key_total = key_all.shape[0]
    queries = query_rows.reshape(row_count, head_count, head_size)

    def key_slices(block_start, piece_size):
        key_block = key_all.reshape(piece_size, head_count, head_size)
        value_block = value_all.reshape(piece_size, head_count, head_size)
        key_pos = block_start + jnp.arange(piece_size, dtype=jnp.int32)
        return (key_block, value_block, key_pos)

    def forward_kernel(running, block_start, piece_size):
        key_block, value_block, key_pos = key_slices(block_start, piece_size)
        return running + forward_part(
            queries, key_block, value_block, cycle_pos, query_first, query_length, key_pos
        )

    zeros_local = jnp.zeros((row_count, head_count, head_size), jnp.float32)
    attention = sweep(forward_kernel, zeros_local, key_total, key_total, lowest, highest).reshape(
        row_count, model_width
    )
    attn_norm, inv_attn = normalize(attention)
    mixed = attn_norm * gate_rows.astype(jnp.float32)
    output = embedded + jnp.dot(
        mixed.astype(jnp.bfloat16), output_weight, preferred_element_type=jnp.float32
    )
    layer_out = output.astype(jnp.bfloat16)
    grad_mixed = jnp.einsum(
        "rk,dk->rd", cotangent, output_weight, preferred_element_type=jnp.float32
    )
    grad_gate = grad_mixed * attn_norm
    grad_attn = normalize_back(
        grad_mixed * gate_rows.astype(jnp.float32), attn_norm, inv_attn
    ).astype(jnp.bfloat16)
    grad_heads = grad_attn.reshape(row_count, head_count, head_size)
    zeros_all = jnp.zeros((key_total, head_count, head_size), jnp.float32)

    def backward_kernel(running, block_start, piece_size):
        key_block, value_block, key_pos = key_slices(block_start, piece_size)
        grad_query, grad_key, grad_value = backward_part(
            queries,
            key_block,
            value_block,
            grad_heads,
            cycle_pos,
            query_first,
            query_length,
            key_pos,
        )
        return (running[0] + grad_query, grad_key, grad_value)

    grad_query, grad_key_all, grad_value_all = sweep(
        backward_kernel, (zeros_local, zeros_all, zeros_all), key_total, key_total, lowest, highest
    )
    grad_key, grad_value = (
        lax.psum_scatter(
            grad_key_all.reshape(key_total, model_width), "cp", scatter_dimension=0, tiled=True
        ),
        lax.psum_scatter(
            grad_value_all.reshape(key_total, model_width), "cp", scatter_dimension=0, tiled=True
        ),
    )
    grad_act = jnp.concatenate(
        [grad_gate, grad_value, grad_query.reshape(row_count, model_width), grad_key], axis=1
    )
    sigmoid_part = jax.nn.sigmoid(projected)
    grad_proj = (grad_act * sigmoid_part * (1.0 + projected * (1.0 - sigmoid_part))).astype(
        jnp.bfloat16
    )
    grad_norm = jnp.einsum("rk,dk->rd", grad_proj, input_weight, preferred_element_type=jnp.float32)
    grad_embed = cotangent.astype(jnp.float32) + normalize_back(grad_norm, normed, inv_embed)
    outgoing = jnp.zeros((devices * capacity, model_width), jnp.float32).at[placed].set(grad_embed)
    arrived = lax.all_to_all(
        outgoing.reshape(devices, capacity, model_width),
        ("dp", "cp"),
        split_axis=0,
        concat_axis=0,
        tiled=True,
    ).reshape(devices * capacity, model_width)
    summed = (
        jnp.zeros(table_rows.shape, jnp.float32)
        .at[lookup]
        .add(jnp.where(wanted[:, None], arrived, 0.0))
    )
    table_grad = summed * row_scales[:, None]
    return (layer_out, table_grad)


def solution(mesh):
    return jax.shard_map(
        per_device,
        mesh=mesh,
        in_specs=(
            P(("dp", "cp"), None),
            P(("dp", "cp")),
            P(("dp", "cp"), None),
            P(("dp", "cp")),
            P("dp", None),
            P(),
            P(),
            P(("dp", "cp"), None),
        ),
        out_specs=(P(("dp", "cp"), None), P(("dp", "cp"), None)),
        check_vma=False,
    )
```

profile of v0, /device:TPU:1, one launch (start us, length us, event | category | flops | bytes accessed | tf_op | source)
XLA Modules:
  0.0 501.4 jit_solution(9689500098973985464)
XLA Ops:
  11.5 20.8 %all_to_all.19 = s32[128,1,2]{2,1,0:T(1,128)S(1)} all-to-all(s32[128,1,2]{2,1,0:T(1,128)S(1)} %bitcast.137), channel_id=1, replica_groups=mesh['dp'=8,'cp'=16] {'dp','cp'}, dimensions={0} | all-to-all | bytes 2048 | tf_op jit(solution)/shard_map/all_to_all | solution.py:112
  35.3 5.1 %gather_fusion = bf16[256,1024]{1,0:T(8,128)(2,1)} fusion(bf16[2048,1024]{1,0:T(8,128)(2,1)} %param.12, s32[1024]{0:T(1024)S(1)} %pad_clamp_fusion.1), kind=kCustom, calls=%fused_computation | custom fusion | bytes 1049600 | tf_op jit(solution)/shard_map/gather | solution.py:118
  43.6 5.6 %all-to-all-start.1 = ((f32[128,2,1024]{2,1,0:T(2,128)}), f32[128,2,1024]{2,1,0:T(2,128)}, u32[]{:S(2)}, u32[]{:S(2)}) async-start(f32[128,2,1024]{2,1,0:T(2,128)} %multiply_select_fusion), calls=%async_computation.1 | async-start | bytes 2097152 | tf_op jit(solution)/shard_map/all_to_all | solution.py:120
  49.2 18.6 %all-to-all-done.1 = f32[128,2,1024]{2,1,0:T(2,128)} async-done(((f32[128,2,1024]{2,1,0:T(2,128)}), f32[128,2,1024]{2,1,0:T(2,128)}, u32[]{:S(2)}, u32[]{:S(2)}) %all-to-all-start.1) | async-done | bytes 1048608 | tf_op jit(solution)/shard_map/all_to_all | solution.py:120
  73.8 6.3 %multiply_convert_fusion = (bf16[128,4096]{1,0:T(8,128)(2,1)S(1)}, f32[128,4096]{1,0:T(8,128)}) fusion(bf16[1024,4096]{1,0:T(8,128)(2,1)} %param.17, f32[128,1024]{1,0:T(8,128)} %gather_fusion.2, f32[128]{0:T(128)S(1)} %add_rsqrt_fusion.1, f32[128]{0:T(128)S(1)} %broadcast_multiply_fusion.6), kind=kOutput, calls=%fused_computation.60 | convolution fusion | flops 1076756480 | bytes 12059648 | tf_op jit(solution)/shard_map/dot_general | solution.py:129
  85.7 49.2 %all-gather.5.cloned.1.call-done = bf16[2048,1024]{1,0:T(8,128)(2,1)} async-done(((bf16[128,1024]{1,0:T(8,128)(2,1)}), bf16[2048,1024]{1,0:T(8,128)(2,1)}) %all-gather.5.cloned.1.call-update) | async-done | bytes 4194320 | tf_op jit(solution)/shard_map/all_gather | solution.py:144
  134.9 57.9 %all-gather.3.cloned.1.call-done = bf16[2048,1024]{1,0:T(8,128)(2,1)} async-done(((bf16[128,1024]{1,0:T(8,128)(2,1)}), bf16[2048,1024]{1,0:T(8,128)(2,1)}) %all-gather.3.cloned.1.call-update) | async-done | bytes 4194320 | tf_op jit(solution)/shard_map/all_gather | solution.py:143
  192.9 8.3 %conditional.2 = (f32[128,8,128]{2,0,1:T(8,128)S(1)}) conditional(s32[]{:T(128)} %convert_element_type.56, f32[128,8,128]{2,0,1:T(8,128)S(1)} %broadcast_in_dim.116, (s32[128]{0:T(128)S(1)}, s32[128]{0:T(128)S(1)}, bf16[2048,1024]{1,0:T(8,128)(2,1)}, bf16[128,8,128]{2,1,0:T(8,128)(2,1)S(1)}, f32[128]{0:T(128)S(1)}, ...), branch_computations={%region_9.10_spmd, %region_10.11_spmd} | conditional | flops 1091436544 | bytes 10225160 | solution.py:80
  194.2 7.0 %fusion.8 = f32[128,8,128]{2,0,1:T(8,128)S(1)} fusion(f32[128,8,128]{2,0,1:T(8,128)S(1)} %get-tuple-element.88, f32[128]{0:T(128)S(1)} %get-tuple-element.116, pred[128,2048]{1,0:T(8,128)(4,1)} %fusion.13, bf16[128,8,128]{2,1,0:T(8,128)(2,1)S(1)} %get-tuple-element.214, bf16[2048,1024]{1,0:T(8,128)(2,1)} %get-tuple-element.117, ...), kind=kOutput, calls=%fused_computation.15 | convolution fusion | flops 1090650112 | bytes 9961984 | tf_op jit(solution)/shard_map/while/body/eval_jaxpr/cond/branch_1_fun/hqk,khe->qhe/dot_general | solution.py:48
  205.7 22.3 %conditional.3 = (f32[2048,8,128]{2,0,1:T(8,128)}, f32[2048,8,128]{2,0,1:T(8,128)S(1)}, f32[128,8,128]{2,0,1:T(8,128)S(1)}) conditional(s32[]{:T(128)} %convert_element_type.56, f32[128,8,128]{2,0,1:T(8,128)S(1)} %broadcast_in_dim.116, (s32[128]{0:T(128)S(1)}, s32[128]{0:T(128)S(1)}, bf16[128,1024]{1,0:T(8,128)(2,1)S(1)}, ...), branch_computations={%region_15.16_spmd, %region_16.17_spmd} | conditional | flops 2729312256 | bytes 103549008 | solution.py:80
  208.4 5.5 %select_convert_fusion.2 = bf16[8,128,2048]{2,1,0:T(8,128)(2,1)S(1)} fusion(f32[8,128,2048]{2,1,0:T(8,128)S(1)} %fusion.21, f32[128]{0:T(128)S(1)} %get-tuple-element.124, pred[128,2048]{1,0:T(8,128)(4,1)S(1)} %fusion.37, bf16[2048,1024]{1,0:T(8,128)(2,1)S(1)} %copy-done.9, bf16[128,1024]{1,0:T(8,128)(2,1)S(1)} %get-tuple-element.120), kind=kOutput, calls=%fused_computation.22 | convolution fusion | flops 564133888 | bytes 17302016 | tf_op jit(solution)/shard_map/while/body/eval_jaxpr/cond/branch_1_fun/qhe,khe->hqk/dot_general | solution.py:59
  217.3 3.7 convolution_bitcast_fusion
  221.0 7.0 %convolution_bitcast_fusion.1 = f32[2048,8,128]{2,0,1:T(8,128)} fusion(bf16[8,128,2048]{2,1,0:T(8,128)(2,1)} %copy-done.5, bf16[128,8,128]{2,1,0:T(8,128)(2,1)S(1)} %get-tuple-element.223), kind=kOutput, calls=%fused_computation.25 | convolution fusion | flops 536870912 | bytes 12845056 | tf_op jit(solution)/shard_map/while/body/eval_jaxpr/cond/branch_1_fun/hqk,qhe->khe/dot_general | solution.py:70
  228.0 4.4 copy_bitcast_fusion.1
  232.7 7.8 %copy_bitcast_fusion = f32[2048,1024]{1,0:T(8,128)} fusion(f32[2048,8,128]{2,0,1:T(8,128)} %get-tuple-element.148), kind=kLoop, calls=%fused_computation.52 | loop fusion | bytes 16777216 | tf_op jit(solution)/shard_map/reshape | solution.py:200
  242.5 89.3 %reduce-scatter.3.cloned.1.call-done = f32[128,1024]{1,0:T(8,128)} async-done(((f32[2048,1024]{1,0:T(8,128)}), f32[128,1024]{1,0:T(8,128)}) %reduce-scatter.3.cloned.1.call-update) | async-done | bytes 524304 | tf_op jit(solution)/shard_map/reduce_scatter | solution.py:202
  331.8 105.4 %reduce-scatter.5.cloned.1.call-done = f32[128,1024]{1,0:T(8,128)} async-done(((f32[2048,1024]{1,0:T(8,128)}), f32[128,1024]{1,0:T(8,128)}) %reduce-scatter.5.cloned.1.call-update) | async-done | bytes 524304 | tf_op jit(solution)/shard_map/reduce_scatter | solution.py:199
  437.2 8.4 %fusion.90 = (f32[128]{0:T(128)S(1)}, f32[128]{0:T(128)S(1)}, f32[128,1024]{1,0:T(8,128)}) fusion(f32[128]{0:T(128)S(1)} %add_rsqrt_fusion.1, f32[128,1024]{1,0:T(8,128)S(1)} %copy-done.2, f32[128]{0:T(128)S(1)} %broadcast_multiply_fusion.6, bf16[1024,4096]{1,0:T(8,128)(2,1)} %param.17, f32[128,1024]{1,0:T(8,128)} %reduce-scatter.5.cloned.1.call-done, ...), kind=kOutput, calls=%fused_computation.132 | convolution fusion | flops 1080688384 | bytes 13633536 | tf_op jit(solution)/shard_map/rk,dk->rd/dot_general | solution.py:213
  445.6 2.7 scatter_custom_fusion.1
  448.3 2.9 reshape.284
  451.2 9.1 %all-to-all-start.2 = ((f32[128,2,1024]{2,1,0:T(2,128)}), f32[128,2,1024]{2,1,0:T(2,128)}, u32[]{:S(2)}, u32[]{:S(2)}) async-start(f32[128,2,1024]{2,1,0:T(2,128)} %reshape.284), calls=%async_computation.4 | async-start | bytes 2097152 | tf_op jit(solution)/shard_map/all_to_all | solution.py:216
  462.6 16.3 %all-to-all-done.2 = f32[128,2,1024]{2,1,0:T(2,128)} async-done(((f32[128,2,1024]{2,1,0:T(2,128)}), f32[128,2,1024]{2,1,0:T(2,128)}, u32[]{:S(2)}, u32[]{:S(2)}) %all-to-all-start.2) | async-done | bytes 1048608 | tf_op jit(solution)/shard_map/all_to_all | solution.py:216
  480.9 6.6 %scatter_custom_fusion.2 = f32[2048,1024]{1,0:T(8,128)} fusion(s32[256]{0:T(256)S(1)} %reshape.290, f32[]{:T(128)} %constant.69.clone.1, f32[256,1024]{1,0:T(8,128)S(1)} %reshape.285, pred[256]{0:T(512)(128)(4,1)S(1)} %gt.23), kind=kCustom, calls=%fused_computation.55 | custom fusion | flops 524288 | bytes 9438720 | tf_op jit(solution)/shard_map/scatter-add | solution.py:226
  487.5 7.4 %broadcast_multiply_fusion = f32[2048,1024]{1,0:T(8,128)} fusion(f32[2048,1024]{1,0:T(8,128)} %scatter_custom_fusion.2, f32[2048]{0:T(1024)S(1)} %copy-done.1), kind=kLoop, calls=%fused_computation.54 | loop fusion | flops 2097152 | bytes 16785408 | tf_op jit(solution)/shard_map/mul | solution.py:228
  (79 shorter events, 38.9 us)
Async XLA Ops:
  7.2 194.4 %copy-start = (bf16[1024,1024]{1,0:T(8,128)(2,1)S(1)}, bf16[1024,1024]{1,0:T(8,128)(2,1)}, u32[]{:S(2)}) copy-start(bf16[1024,1024]{1,0:T(8,128)(2,1)} %param.18) | copy-start | bytes 6291460
  43.6 24.3 %all-to-all-start.1 = ((f32[128,2,1024]{2,1,0:T(2,128)}), f32[128,2,1024]{2,1,0:T(2,128)}, u32[]{:S(2)}, u32[]{:S(2)}) async-start(f32[128,2,1024]{2,1,0:T(2,128)} %multiply_select_fusion), calls=%async_computation.1 | async-start | bytes 2097152 | tf_op jit(solution)/shard_map/all_to_all | solution.py:120
  49.2 85.7 %all-gather.5.cloned.1.call-start = ((), (), s32[]{:S(2)}) async-start(), calls=%async_computation.6 | async-start | bytes 4456448 | tf_op jit(solution)/shard_map/all_gather | solution.py:144
  73.8 9.6 %copy-start.8 = (s32[1,3]{1,0:T(1,128)S(1)}, s32[1,3]{1,0:T(1,128)}, u32[]{:S(2)}) copy-start(s32[1,3]{1,0:T(1,128)} %param.16) | copy-start | bytes 40
  80.2 1.0 copy-start.6
  82.0 110.8 %all-gather.3.cloned.1.call-start = ((), (), s32[]{:S(2)}) async-start(), calls=%async_computation.5 | async-start | bytes 4456448 | tf_op jit(solution)/shard_map/all_gather | solution.py:143
  82.8 249.0 %reduce-scatter.3.cloned.1.call-start = ((), (), s32[]{:S(2)}) async-start(), calls=%async_computation.7 | async-start | bytes 8912896 | tf_op jit(solution)/shard_map/reduce_scatter | solution.py:202
  201.3 4.4 copy-start.4
  206.2 2.2 copy-start.9
  213.8 2.0 copy-start.5
  228.0 4.4 copy-start.3
  232.4 204.8 %reduce-scatter.5.cloned.1.call-start = ((), (), s32[]{:S(2)}) async-start(), calls=%async_computation.8 | async-start | bytes 8912896 | tf_op jit(solution)/shard_map/reduce_scatter | solution.py:199
  240.5 196.7 %copy-start.2 = (f32[128,1024]{1,0:T(8,128)S(1)}, f32[128,1024]{1,0:T(8,128)}, u32[]{:S(2)}) copy-start(f32[128,1024]{1,0:T(8,128)} %gather_fusion.2) | copy-start | bytes 1572868
  437.2 8.4 %copy-start.7 = (bf16[128,1024]{1,0:T(8,128)(2,1)S(1)}, bf16[128,1024]{1,0:T(8,128)(2,1)}, u32[]{:S(2)}) copy-start(bf16[128,1024]{1,0:T(8,128)(2,1)} %param.19) | copy-start | bytes 786436
  451.2 27.7 %all-to-all-start.2 = ((f32[128,2,1024]{2,1,0:T(2,128)}), f32[128,2,1024]{2,1,0:T(2,128)}, u32[]{:S(2)}, u32[]{:S(2)}) async-start(f32[128,2,1024]{2,1,0:T(2,128)} %reshape.284), calls=%async_computation.4 | async-start | bytes 2097152 | tf_op jit(solution)/shard_map/all_to_all | solution.py:216
  480.8 6.7 %copy-start.1 = (f32[2048]{0:T(1024)S(1)}, f32[2048]{0:T(1024)}, u32[]{:S(2)}) copy-start(f32[2048]{0:T(1024)} %param.13) | copy-start | bytes 24580
Sparse Core Ops, SparseCore 0:
  82.1 52.7 all-gather.4
  137.9 54.9 all-gather.2
  232.5 99.2 reduce-scatter.2
  336.0 101.1 reduce-scatter.4
where the time goes:
time: 502 us; the launch traced here: 501 us
  waiting for transfers between devices  337 us (67%)
  matrix products  44.9 us (9%)
  local copies, waits for them, and re-layouts  38.4 us (8%)
  other arithmetic  29.3 us (6%)
  blocking collectives  20.8 us (4%)
  between operations  15.3 us (3%)
  starting transfers between devices  15.1 us (3%)
    reduce_scatter x1, waiting for transfers between devices, per_device(): lax.psum_scatter(grad_key_all.reshape(key_total, model_width), 'cp', scat...  105 us
    reduce_scatter x1, waiting for transfers between devices, per_device(): lax.psum_scatter(grad_value_all.reshape(key_total, model_width), 'cp', sc...  89.3 us
    all_gather x1, waiting for transfers between devices, per_device(): lax.all_gather(key_rows, 'cp', axis=0, tiled=True)  57.9 us
    all_gather x1, waiting for transfers between devices, per_device(): lax.all_gather(value_rows, 'cp', axis=0, tiled=True)  49.2 us
    all_to_all x1, blocking collectives, per_device(): lax.all_to_all(requests.reshape(devices, capacity), ('dp', 'cp'), split_a...  20.8 us
    all_to_all x1, waiting for transfers between devices, per_device(): lax.all_to_all(fetched.reshape(devices, capacity, model_width), ('dp', 'c...  18.6 us
    all_to_all x1, waiting for transfers between devices, per_device(): lax.all_to_all(outgoing.reshape(devices, capacity, model_width), ('dp', '...  16.3 us
  transfers between devices with their start and end apart: 6, of which 6 were waited for; matrix products, arithmetic and copies ran while one was open for 3% of the time, Pallas kernels for 0%

commit v1 on v0

--- a/solution.py
+++ b/solution.py
@@ -140,7 +140,9 @@
     lowest = jnp.min(query_first)
     highest = cycle_pos[row_count - 1]
     key_all, value_all = (
-        lax.all_gather(key_rows, "cp", axis=0, tiled=True),
+        jnp.concatenate(
+            lax.all_to_all(jnp.stack([key_rows] * lax.axis_size("cp")), "cp", 0, 0), axis=0
+        ),
         lax.all_gather(value_rows, "cp", axis=0, tiled=True),
     )
     key_total = key_all.shape[0]

time: 502 us -> 493 us (0.982); the launches traced: 501 us -> 484 us
  waiting for transfers between devices: 337 us -> 301 us
  local copies, waits for them, and re-layouts: 38.4 us -> 49.3 us
  starting transfers between devices: 15.1 us -> 20.4 us
    all_to_all x0 -> x1, waiting for transfers between devices: none -> 62.4 us  [per_device(): lax.all_to_all(jnp.stack([key_rows] * lax.axis_size('cp')), 'cp', 0, 0)]
    all_gather x1 -> x0, waiting for transfers between devices: 57.9 us -> none  [per_device(): lax.all_gather(key_rows, 'cp', axis=0, tiled=True)]
    all_gather x1, waiting for transfers between devices: 49.2 us -> 8.54 us  [per_device(): lax.all_gather(value_rows, 'cp', axis=0, tiled=True)]
    cond x4 -> x6, local copies, waits for them, and re-layouts: 2.84 us -> 11.4 us
    all_to_all x0 -> x1, starting transfers between devices: none -> 5.43 us  [per_device(): lax.all_to_all(jnp.stack([key_rows] * lax.axis_size('cp')), 'cp', 0, 0)]
where the time goes in v1:
time: 493 us; the launch traced here: 484 us
  waiting for transfers between devices  301 us (61%)
  local copies, waits for them, and re-layouts  49.3 us (10%)
  matrix products  47 us (10%)
  other arithmetic  29.3 us (6%)
  blocking collectives  20.8 us (4%)
  starting transfers between devices  20.4 us (4%)
  between operations  15.5 us (3%)
    reduce_scatter x1, waiting for transfers between devices, per_device(): lax.psum_scatter(grad_key_all.reshape(key_total, model_width), 'cp', scat...  106 us
    reduce_scatter x1, waiting for transfers between devices, per_device(): lax.psum_scatter(grad_value_all.reshape(key_total, model_width), 'cp', sc...  89.9 us
    all_to_all x1, waiting for transfers between devices, per_device(): lax.all_to_all(jnp.stack([key_rows] * lax.axis_size('cp')), 'cp', 0, 0)  62.4 us
    all_to_all x1, blocking collectives, per_device(): lax.all_to_all(requests.reshape(devices, capacity), ('dp', 'cp'), split_a...  20.8 us
    all_to_all x1, waiting for transfers between devices, per_device(): lax.all_to_all(fetched.reshape(devices, capacity, model_width), ('dp', 'c...  18.6 us
    all_to_all x1, waiting for transfers between devices, per_device(): lax.all_to_all(outgoing.reshape(devices, capacity, model_width), ('dp', '...  16.3 us
    cond x6, local copies, waits for them, and re-layouts  11.4 us
  transfers between devices with their start and end apart: 6, of which 6 were waited for; matrix products, arithmetic and copies ran while one was open for 3% of the time, Pallas kernels for 0%

profile of v1, /device:TPU:1, one launch (start us, length us, event | category | flops | bytes accessed | tf_op | source)
XLA Modules:
  0.0 484.3 jit_solution(3061758293601893756)
XLA Ops:
  11.5 20.8 %all_to_all.24 = s32[128,1,2]{2,1,0:T(1,128)S(1)} all-to-all(s32[128,1,2]{2,1,0:T(1,128)S(1)} %bitcast.120), channel_id=1, replica_groups=mesh['dp'=8,'cp'=16] {'dp','cp'}, dimensions={0} | all-to-all | bytes 2048 | tf_op jit(solution)/shard_map/all_to_all | solution.py:112
  35.3 5.1 %gather_fusion = bf16[256,1024]{1,0:T(8,128)(2,1)} fusion(bf16[2048,1024]{1,0:T(8,128)(2,1)} %param.12, s32[1024]{0:T(1024)S(1)} %pad_clamp_fusion.1), kind=kCustom, calls=%fused_computation | custom fusion | bytes 1049600 | tf_op jit(solution)/shard_map/gather | solution.py:118
  43.6 5.6 %all-to-all-start.1 = ((f32[128,2,1024]{2,1,0:T(2,128)}), f32[128,2,1024]{2,1,0:T(2,128)}, u32[]{:S(2)}, u32[]{:S(2)}) async-start(f32[128,2,1024]{2,1,0:T(2,128)} %multiply_select_fusion), calls=%async_computation.1 | async-start | bytes 2097152 | tf_op jit(solution)/shard_map/all_to_all | solution.py:120
  49.2 18.6 %all-to-all-done.1 = f32[128,2,1024]{2,1,0:T(2,128)} async-done(((f32[128,2,1024]{2,1,0:T(2,128)}), f32[128,2,1024]{2,1,0:T(2,128)}, u32[]{:S(2)}, u32[]{:S(2)}) %all-to-all-start.1) | async-done | bytes 1048608 | tf_op jit(solution)/shard_map/all_to_all | solution.py:120
  73.8 6.3 %multiply_convert_fusion = (bf16[128,4096]{1,0:T(8,128)(2,1)S(1)}, f32[128,4096]{1,0:T(8,128)}) fusion(bf16[1024,4096]{1,0:T(8,128)(2,1)} %param.17, f32[128,1024]{1,0:T(8,128)} %gather_fusion.2, f32[128]{0:T(128)S(1)} %add_rsqrt_fusion.1, f32[128]{0:T(128)S(1)} %broadcast_multiply_fusion.6), kind=kOutput, calls=%fused_computation.57 | convolution fusion | flops 1076756480 | bytes 12059648 | tf_op jit(solution)/shard_map/dot_general | solution.py:129
  84.5 5.4 %all-to-all-start.2 = ((bf16[16,128,1024]{2,1,0:T(8,128)(2,1)}), bf16[16,128,1024]{2,1,0:T(8,128)(2,1)}, u32[]{:S(2)}, u32[]{:S(2)}) async-start(bf16[16,128,1024]{2,1,0:T(8,128)(2,1)} %stack.2), calls=%async_computation.2 | async-start | bytes 8388608 | tf_op jit(solution)/shard_map/all_to_all | solution.py:144
  92.8 62.4 %all-to-all-done.2 = bf16[16,128,1024]{2,1,0:T(8,128)(2,1)} async-done(((bf16[16,128,1024]{2,1,0:T(8,128)(2,1)}), bf16[16,128,1024]{2,1,0:T(8,128)(2,1)}, u32[]{:S(2)}, u32[]{:S(2)}) %all-to-all-start.2) | async-done | bytes 4194336 | tf_op jit(solution)/shard_map/all_to_all | solution.py:144
  155.2 8.5 %all-gather.2.cloned.1.call-done = bf16[2048,1024]{1,0:T(8,128)(2,1)} async-done(((bf16[128,1024]{1,0:T(8,128)(2,1)}), bf16[2048,1024]{1,0:T(8,128)(2,1)}) %all-gather.2.cloned.1.call-update) | async-done | bytes 4194320 | tf_op jit(solution)/shard_map/all_gather | solution.py:146
  163.8 15.7 %conditional.2 = (f32[128,8,128]{2,0,1:T(8,128)S(1)}) conditional(s32[]{:T(128)} %convert_element_type.56, f32[128,8,128]{2,0,1:T(8,128)S(1)} %broadcast_in_dim.116, (s32[128]{0:T(128)S(1)}, s32[128]{0:T(128)S(1)}, bf16[16,128,1024]{2,1,0:T(8,128)(2,1)}, bf16[128,8,128]{2,1,0:T(8,128)(2,1)S(1)}, f32[128]{0:T(128)S(1)}, ...), branch_computations={%region_9.10_spmd, %region_10.11_spmd} | conditional | flops 1091436544 | bytes 18613768 | solution.py:80
  165.5 5.3 %copy.95 = bf16[256,8,8,128]{3,2,1,0:T(8,128)(2,1)} copy(bf16[256,8,8,128]{3,1,2,0:T(8,128)(2,1)} %bitcast.18) | data formatting | bytes 8388608 | tf_op jit(solution)/shard_map/while/body/eval_jaxpr/cond
  170.8 8.8 %fusion.7 = f32[128,8,128]{2,0,1:T(8,128)S(1)} fusion(f32[128,8,128]{2,0,1:T(8,128)S(1)} %get-tuple-element.88, bf16[2048,8,128]{2,1,0:T(8,128)(2,1)} %bitcast.117, f32[128]{0:T(128)S(1)} %get-tuple-element.116, pred[128,2048]{1,0:T(8,128)(4,1)} %fusion.12, bf16[128,8,128]{2,1,0:T(8,128)(2,1)S(1)} %get-tuple-element.214, ...), kind=kOutput, calls=%fused_computation.14 | convolution fusion | flops 1090650112 | bytes 9961984 | tf_op jit(solution)/shard_map/while/body/eval_jaxpr/cond/branch_1_fun/hqk,khe->qhe/dot_general | solution.py:48
  183.9 26.1 %conditional.3 = (f32[2048,8,128]{2,0,1:T(8,128)}, f32[2048,8,128]{2,0,1:T(8,128)S(1)}, f32[128,8,128]{2,0,1:T(8,128)S(1)}) conditional(s32[]{:T(128)} %convert_element_type.56, f32[128,8,128]{2,0,1:T(8,128)S(1)} %broadcast_in_dim.116, (s32[128]{0:T(128)S(1)}, s32[128]{0:T(128)S(1)}, bf16[128,1024]{1,0:T(8,128)(2,1)S(1)}, ...), branch_computations={%region_15.16_spmd, %region_16.17_spmd} | conditional | flops 2729312256 | bytes 111937616 | solution.py:80
  190.0 5.5 %select_convert_fusion.2 = bf16[8,128,2048]{2,1,0:T(8,128)(2,1)S(1)} fusion(f32[8,128,2048]{2,1,0:T(8,128)S(1)} %fusion.26, f32[128]{0:T(128)S(1)} %get-tuple-element.124, pred[128,2048]{1,0:T(8,128)(4,1)S(1)} %fusion.34, bf16[2048,1024]{1,0:T(8,128)(2,1)S(1)} %copy-done.8, bf16[128,1024]{1,0:T(8,128)(2,1)S(1)} %get-tuple-element.120), kind=kOutput, calls=%fused_computation.21 | convolution fusion | flops 564133888 | bytes 17302016 | tf_op jit(solution)/shard_map/while/body/eval_jaxpr/cond/branch_1_fun/qhe,khe->hqk/dot_general | solution.py:59
  199.3 3.7 convolution_bitcast_fusion
  203.0 7.0 %convolution_bitcast_fusion.1 = f32[2048,8,128]{2,0,1:T(8,128)} fusion(bf16[8,128,2048]{2,1,0:T(8,128)(2,1)} %copy-done.4, bf16[128,8,128]{2,1,0:T(8,128)(2,1)S(1)} %get-tuple-element.223), kind=kOutput, calls=%fused_computation.24 | convolution fusion | flops 536870912 | bytes 12845056 | tf_op jit(solution)/shard_map/while/body/eval_jaxpr/cond/branch_1_fun/hqk,qhe->khe/dot_general | solution.py:70
  210.0 4.4 copy_bitcast_fusion.1
  214.7 7.8 %copy_bitcast_fusion = f32[2048,1024]{1,0:T(8,128)} fusion(f32[2048,8,128]{2,0,1:T(8,128)} %get-tuple-element.148), kind=kLoop, calls=%fused_computation.49 | loop fusion | bytes 16777216 | tf_op jit(solution)/shard_map/reshape | solution.py:202
  224.5 89.9 %reduce-scatter.3.cloned.1.call-done = f32[128,1024]{1,0:T(8,128)} async-done(((f32[2048,1024]{1,0:T(8,128)}), f32[128,1024]{1,0:T(8,128)}) %reduce-scatter.3.cloned.1.call-update) | async-done | bytes 524304 | tf_op jit(solution)/shard_map/reduce_scatter | solution.py:204
  314.4 105.5 %reduce-scatter.5.cloned.1.call-done = f32[128,1024]{1,0:T(8,128)} async-done(((f32[2048,1024]{1,0:T(8,128)}), f32[128,1024]{1,0:T(8,128)}) %reduce-scatter.5.cloned.1.call-update) | async-done | bytes 524304 | tf_op jit(solution)/shard_map/reduce_scatter | solution.py:201
  419.9 8.4 %fusion.87 = (f32[128]{0:T(128)S(1)}, f32[128]{0:T(128)S(1)}, f32[128,1024]{1,0:T(8,128)}) fusion(f32[128]{0:T(128)S(1)} %add_rsqrt_fusion.1, f32[128,1024]{1,0:T(8,128)S(1)} %copy-done.2, f32[128]{0:T(128)S(1)} %broadcast_multiply_fusion.6, bf16[1024,4096]{1,0:T(8,128)(2,1)} %param.17, f32[128,1024]{1,0:T(8,128)} %reduce-scatter.5.cloned.1.call-done, ...), kind=kOutput, calls=%fused_computation.129 | convolution fusion | flops 1080688384 | bytes 13633536 | tf_op jit(solution)/shard_map/rk,dk->rd/dot_general | solution.py:215
  433.9 9.1 %all-to-all-start.3 = ((f32[128,2,1024]{2,1,0:T(2,128)}), f32[128,2,1024]{2,1,0:T(2,128)}, u32[]{:S(2)}, u32[]{:S(2)}) async-start(f32[128,2,1024]{2,1,0:T(2,128)} %reshape.280), calls=%async_computation.5 | async-start | bytes 2097152 | tf_op jit(solution)/shard_map/all_to_all | solution.py:218
  445.3 16.3 %all-to-all-done.3 = f32[128,2,1024]{2,1,0:T(2,128)} async-done(((f32[128,2,1024]{2,1,0:T(2,128)}), f32[128,2,1024]{2,1,0:T(2,128)}, u32[]{:S(2)}, u32[]{:S(2)}) %all-to-all-start.3) | async-done | bytes 1048608 | tf_op jit(solution)/shard_map/all_to_all | solution.py:218
  463.5 6.6 %scatter_custom_fusion.2 = f32[2048,1024]{1,0:T(8,128)} fusion(s32[256]{0:T(256)S(1)} %reshape.286, f32[]{:T(128)} %constant.69.clone.1, f32[256,1024]{1,0:T(8,128)S(1)} %reshape.281, pred[256]{0:T(512)(128)(4,1)S(1)} %gt.23), kind=kCustom, calls=%fused_computation.52 | custom fusion | flops 524288 | bytes 9438720 | tf_op jit(solution)/shard_map/scatter-add | solution.py:228
  470.2 7.4 %broadcast_multiply_fusion = f32[2048,1024]{1,0:T(8,128)} fusion(f32[2048,1024]{1,0:T(8,128)} %scatter_custom_fusion.2, f32[2048]{0:T(1024)S(1)} %copy-done.1), kind=kLoop, calls=%fused_computation.51 | loop fusion | flops 2097152 | bytes 16785408 | tf_op jit(solution)/shard_map/mul | solution.py:230
  (79 shorter events, 49.8 us)
Async XLA Ops:
  7.2 172.7 %copy-start = (bf16[1024,1024]{1,0:T(8,128)(2,1)S(1)}, bf16[1024,1024]{1,0:T(8,128)(2,1)}, u32[]{:S(2)}) copy-start(bf16[1024,1024]{1,0:T(8,128)(2,1)} %param.18) | copy-start | bytes 6291460
  43.6 24.3 %all-to-all-start.1 = ((f32[128,2,1024]{2,1,0:T(2,128)}), f32[128,2,1024]{2,1,0:T(2,128)}, u32[]{:S(2)}, u32[]{:S(2)}) async-start(f32[128,2,1024]{2,1,0:T(2,128)} %multiply_select_fusion), calls=%async_computation.1 | async-start | bytes 2097152 | tf_op jit(solution)/shard_map/all_to_all | solution.py:120
  49.2 114.6 %all-gather.2.cloned.1.call-start = ((), (), s32[]{:S(2)}) async-start(), calls=%async_computation.6 | async-start | bytes 4456448 | tf_op jit(solution)/shard_map/all_gather | solution.py:146
  80.1 1.0 copy-start.5
  80.1 10.4 %copy-start.7 = (s32[1,3]{1,0:T(1,128)S(1)}, s32[1,3]{1,0:T(1,128)}, u32[]{:S(2)}) copy-start(s32[1,3]{1,0:T(1,128)} %param.16) | copy-start | bytes 40
  84.5 70.8 %all-to-all-start.2 = ((bf16[16,128,1024]{2,1,0:T(8,128)(2,1)}), bf16[16,128,1024]{2,1,0:T(8,128)(2,1)}, u32[]{:S(2)}, u32[]{:S(2)}) async-start(bf16[16,128,1024]{2,1,0:T(8,128)(2,1)} %stack.2), calls=%async_computation.2 | async-start | bytes 8388608 | tf_op jit(solution)/shard_map/all_to_all | solution.py:144
  89.9 224.4 %reduce-scatter.3.cloned.1.call-start = ((), (), s32[]{:S(2)}) async-start(), calls=%async_computation.7 | async-start | bytes 8912896 | tf_op jit(solution)/shard_map/reduce_scatter | solution.py:204
  187.8 2.2 copy-start.8
  195.4 2.0 copy-start.4
  210.0 4.7 copy-start.3
  214.4 205.4 %reduce-scatter.5.cloned.1.call-start = ((), (), s32[]{:S(2)}) async-start(), calls=%async_computation.8 | async-start | bytes 8912896 | tf_op jit(solution)/shard_map/reduce_scatter | solution.py:201
  222.5 197.4 %copy-start.2 = (f32[128,1024]{1,0:T(8,128)S(1)}, f32[128,1024]{1,0:T(8,128)}, u32[]{:S(2)}) copy-start(f32[128,1024]{1,0:T(8,128)} %gather_fusion.2) | copy-start | bytes 1572868
  419.9 8.4 %copy-start.6 = (bf16[128,1024]{1,0:T(8,128)(2,1)S(1)}, bf16[128,1024]{1,0:T(8,128)(2,1)}, u32[]{:S(2)}) copy-start(bf16[128,1024]{1,0:T(8,128)(2,1)} %param.19) | copy-start | bytes 786436
  433.9 36.3 %copy-start.1 = (f32[2048]{0:T(1024)S(1)}, f32[2048]{0:T(1024)}, u32[]{:S(2)}) copy-start(f32[2048]{0:T(1024)} %param.13) | copy-start | bytes 24580
  433.9 27.7 %all-to-all-start.3 = ((f32[128,2,1024]{2,1,0:T(2,128)}), f32[128,2,1024]{2,1,0:T(2,128)}, u32[]{:S(2)}, u32[]{:S(2)}) async-start(f32[128,2,1024]{2,1,0:T(2,128)} %reshape.280), calls=%async_computation.5 | async-start | bytes 2097152 | tf_op jit(solution)/shard_map/all_to_all | solution.py:218
Sparse Core Ops, SparseCore 0:
  82.0 81.6 all-gather.1
  214.6 99.7 reduce-scatter.2
  318.7 101.1 reduce-scatter.4
